TPU v7x, 512 devices: a whole 4x4x16 slice. The times are simulated.
512 devices in a mesh: img: 16 (over z_hi, y, core), term: 32 (over z_lo, x).
Axes of the slice: x: 4, y: 4, z: 16 (z_hi: 2, z_lo: 8; z = z_hi * 8 + z_lo), core: 2. Of those that a mesh axis runs over, the one named last changes fastest.
Arguments:
- patches: bfloat16 [64, 256, 1024], P('img', 'term'), may hold values from -6 to 6
- patch_mask: int32 [64, 256], P('img', 'term'), may hold values 0 or 1
- proj_weight: bfloat16 [1024, 30720], P('img', 'term'), may hold values from -0.1875 to 0.1875
- proj_bias: float32 [30720], P('term'), may hold values from -4 to 4
- slab: bfloat16 [8128, 30720], P('img', 'term'), may hold values from 0 to 2
- query_ids: int32 [1024, 32], replicated, may hold values from -1 to 30719, as said below
- term_weights: bfloat16 [1024, 32], replicated, may hold values from 0.25 to 4
Outputs:
- scores: float32 [1024, 8192], P('term', 'img')
Inputs may be any that keep to these rules, and one draw needn't show every extreme that they name: `query_ids`: within a query the non-negative ids are distinct and come before the padding slots; every query has at least 8 real terms and some query fills all 32 slots.
All inputs are finite; a program needn't handle non-finite values. No bound on the sum of `patch_mask` on one device may be relied on, other than what follows from the above.
Results may differ from a plain program's by a relative error of at most 0.0003.
Values may be sent and summed in bfloat16 or wider, within the bound.
A program may use at most 64 MiB of HBM per device.

v0:
```python
import jax
import jax.numpy as jnp
from jax import lax
from jax.sharding import PartitionSpec as P


def shards(patches, patch_mask, proj_weight, proj_bias, slab, query_ids, term_weights):
    proj_full = lax.all_gather(proj_weight, "img", axis=0, tiled=True)
    block_width = proj_full.shape[1]
    start_max = jnp.zeros((patches.shape[0], block_width), jnp.float32)
    features = lax.all_gather(patches, "term", axis=1, tiled=True)
    keep_mask = lax.all_gather(patch_mask.astype(jnp.bfloat16), "term", axis=1, tiled=True)
    logits = (
        jnp.einsum("npd,dv->npv", features, proj_full, preferred_element_type=jnp.float32)
        + proj_bias
    )
    activity = jnp.log1p(jnp.maximum(logits, 0.0))
    activity = jnp.where(keep_mask[:, :, None] > 0, activity, 0.0)
    pooled = jnp.maximum(start_max, jnp.max(activity, axis=1))
    impacts = jnp.concatenate([slab, pooled.astype(jnp.bfloat16)], axis=0)
    zero_value = jnp.zeros((), jnp.bfloat16)
    weights = jnp.where(query_ids >= 0, term_weights, zero_value)
    offset = lax.axis_index("term") * block_width
    columns = offset + lax.iota(jnp.int32, block_width)
    dense_rows = jnp.sum(
        jnp.where(query_ids[:, :, None] == columns[None, None, :], weights[:, :, None], zero_value),
        axis=1,
    )
    return lax.psum_scatter(
        lax.dot_general(
            dense_rows, impacts, (((1,), (1,)), ((), ())), preferred_element_type=jnp.float32
        ),
        "term",
        scatter_dimension=0,
        tiled=True,
    )


def solution(mesh):
    placed = (
        P("img", "term", None),
        P("img", "term"),
        P("img", "term"),
        P("term"),
        P("img", "term"),
        P(),
        P(),
    )
    return jax.shard_map(
        shards, mesh=mesh, in_specs=placed, out_specs=P("term", "img"), check_vma=False
    )
```

profile of v0, /device:TPU:24, one launch (start us, length us, event | category | flops | bytes accessed | tf_op | source)
XLA Modules:
  0.0 582.1 jit_solution(16606816592213149012)
XLA Ops:
  6.5 0.0 copy-start.1
  6.5 0.0 all-gather.6.cloned.1.call-start
  6.5 0.7 all-gather.6.cloned.1.call-update
  7.3 0.0 all-gather.4.cloned.1.call-start
  7.3 0.7 all-gather.4.cloned.1.call-update
  8.0 0.0 reduce-scatter.2.cloned.1.call-start
  8.1 0.7 convert_bitcast_fusion
  8.7 132.7 %all-gather = bf16[32,8,4]{1,2,0:T(4,128)(2,1)S(1)} all-gather(bf16[1,8,4]{1,2,0:T(4,128)(2,1)S(1)} %convert_bitcast_fusion), channel_id=1, replica_groups=mesh['img'=16,'term'=32] {'term'}, dimensions={0}, use_global_device_ids=true | all-gather | bytes 2112 | tf_op jit(solution)/shard_map/all_gather | solution.py:12
  141.4 0.1 copy.23
  141.5 0.1 copy.24
  141.6 0.1 reshape.12
  141.7 1.0 compare_select_fusion.1
  142.7 17.3 %fusion = bf16[1024,960]{0,1:T(8,128)(2,1)S(1)} fusion(s32[1024,32]{0,1:T(8,128)} %param.12, s32[960]{0:T(1024)S(1)} %iota_add_fusion, bf16[1024,32]{0,1:T(8,128)(2,1)S(1)} %compare_select_fusion.1), kind=kLoop, calls=%fused_computation.1 | loop fusion | flops 93388800 | bytes 2166528 | tf_op jit(solution)/shard_map/reduce_sum | solution.py:25
  160.1 0.0 all-gather.6.cloned.1.call-done
  160.1 163.3 %all-gather.4.cloned.1.call-done = bf16[4,256,1024]{2,1,0:T(8,128)(2,1)} async-done(((bf16[4,8,1024]{2,1,0:T(8,128)(2,1)}), bf16[4,256,1024]{2,1,0:T(8,128)(2,1)}) %all-gather.4.cloned.1.call-update) | async-done | bytes 2097168 | tf_op jit(solution)/shard_map/all_gather | solution.py:11
  323.4 0.0 copy-done.1
  323.4 0.0 copy-start
  323.4 6.1 %select_reduce_fusion = bf16[4,960]{1,0:T(4,128)(2,1)S(1)} fusion(f32[960]{0:T(1024)S(1)} %copy-done.1, pred[4,256]{1,0:T(4,128)(4,1)S(1)} %bitcast.14, bf16[4,256,1024]{2,1,0:T(8,128)(2,1)} %all-gather.4.cloned.1.call-done, bf16[1024,960]{1,0:T(8,128)(2,1)} %all-gather.6.cloned.1.call-done), kind=kOutput, calls=%fused_computation.2 | convolution fusion | flops 2017194240 | bytes 4075776 | tf_op jit(solution)/shard_map/npd,dv->npv/dot_general | solution.py:14
  329.5 0.2 copy.25
  329.7 0.0 copy-done
  329.8 2.7 fusion.5
  332.4 0.0 reduce-scatter.2.cloned.1.call-update
  332.5 243.2 %reduce-scatter.2.cloned.1.call-done = f32[32,512]{1,0:T(8,128)} async-done(((f32[1024,512]{1,0:T(8,128)}), f32[32,512]{1,0:T(8,128)}) %reduce-scatter.2.cloned.1.call-update) | async-done | bytes 65552 | tf_op jit(solution)/shard_map/reduce_scatter | solution.py:29
  (3 shorter events, 0.0 us)
Async XLA Ops:
  6.5 316.8 %copy-start.1 = (f32[960]{0:T(1024)S(1)}, f32[960]{0:T(1024)}, u32[]{:S(2)}) copy-start(f32[960]{0:T(1024)} %param.10) | copy-start | bytes 11524
  6.5 153.5 %all-gather.6.cloned.1.call-start = ((), (), s32[]{:S(2)}) async-start(), calls=%async_computation.2 | async-start | bytes 2228224 | tf_op jit(solution)/shard_map/all_gather | solution.py:8
  7.3 316.1 %all-gather.4.cloned.1.call-start = ((), (), s32[]{:S(2)}) async-start(), calls=%async_computation.1 | async-start | bytes 2162688 | tf_op jit(solution)/shard_map/all_gather | solution.py:11
  8.0 567.6 %reduce-scatter.2.cloned.1.call-start = ((), (), s32[]{:S(2)}) async-start(), calls=%async_computation.3 | async-start | bytes 2162688 | tf_op jit(solution)/shard_map/reduce_scatter | solution.py:29
  323.4 6.4 %copy-start = (bf16[508,960]{0,1:T(8,128)(2,1)S(1)}, bf16[508,960]{0,1:T(8,128)(2,1)}, u32[]{:S(2)}) copy-start(bf16[508,960]{0,1:T(8,128)(2,1)} %param.11) | copy-start | bytes 2926084
Sparse Core Ops, SparseCore 0:
  10.6 95.9 all-gather.5
  108.7 214.5 all-gather.3
  332.6 242.9 reduce-scatter.1
where the time goes:
time: 582 us
  waiting for transfers between devices  408 us (70%)
  blocking collectives  133 us (23%)
  other arithmetic  19 us (3%)
  between operations  13.2 us (2%)
  matrix products  8.82 us (2%)
    reduce_scatter x1, waiting for transfers between devices, shards(): lax.psum_scatter(lax.dot_general(dense_rows, impacts, (((1,), (1,)), ((),...  243 us
    all_gather x1, waiting for transfers between devices, shards(): features = lax.all_gather(patches, 'term', axis=1, tiled=True)  163 us
    all_gather x1, blocking collectives, shards(): lax.all_gather(patch_mask.astype(jnp.bfloat16), 'term', axis=1, tiled=True)  133 us
    reduce_sum x1, other arithmetic, shards(): jnp.sum(jnp.where(query_ids[:, :, None] == columns[None, None, :], weight...  17.3 us
  transfers between devices with their start and end apart: 3, of which 2 were waited for; matrix products, arithmetic and copies ran while one was open for 3% of the time, Pallas kernels for 0%

commit v1 on v0

--- a/solution.py
+++ b/solution.py
@@ -8,7 +8,9 @@
     proj_full = lax.all_gather(proj_weight, "img", axis=0, tiled=True)
     block_width = proj_full.shape[1]
     start_max = jnp.zeros((patches.shape[0], block_width), jnp.float32)
-    features = lax.all_gather(patches, "term", axis=1, tiled=True)
+    features = jnp.concatenate(
+        lax.all_to_all(jnp.stack([patches] * lax.axis_size("term")), "term", 0, 0), axis=1
+    )
     keep_mask = lax.all_gather(patch_mask.astype(jnp.bfloat16), "term", axis=1, tiled=True)
     logits = (
         jnp.einsum("npd,dv->npv", features, proj_full, preferred_element_type=jnp.float32)

time: 582 us -> 483 us (0.83)
  waiting for transfers between devices: 408 us -> 252 us
  blocking collectives: 133 us -> 172 us
  starting transfers between devices: 0.08 us -> 15.6 us
    all_gather x1 -> x0, waiting for transfers between devices: 163 us -> none  [shards(): features = lax.all_gather(patches, 'term', axis=1, tiled=True)]
    all_gather x1, blocking collectives: 133 us -> 172 us  [shards(): lax.all_gather(patch_mask.astype(jnp.bfloat16), 'term', axis=1, tiled=True)]
    all_to_all x0 -> x1, starting transfers between devices: none -> 15.5 us  [shards(): lax.all_to_all(jnp.stack([patches] * lax.axis_size('term')), 'term', 0, 0)]
    reduce_scatter x1, waiting for transfers between devices: 243 us -> 251 us  [shards(): lax.psum_scatter(lax.dot_general(dense_rows, impacts, (((1,), (1,)), ((),...]
  transfers between devices with their start and end apart: 3 -> 3, of which waited for: 2 -> 1; matrix products, arithmetic and copies ran while one was open for 3% -> 4% of each run, Pallas kernels for 0% -> 0%
where the time goes in v1:
time: 483 us
  waiting for transfers between devices  252 us (52%)
  blocking collectives  172 us (36%)
  other arithmetic  17.4 us (4%)
  starting transfers between devices  15.6 us (3%)
  between operations  13.5 us (3%)
  matrix products  9.73 us (2%)
    reduce_scatter x1, waiting for transfers between devices, shards(): lax.psum_scatter(lax.dot_general(dense_rows, impacts, (((1,), (1,)), ((),...  251 us
    all_gather x1, blocking collectives, shards(): lax.all_gather(patch_mask.astype(jnp.bfloat16), 'term', axis=1, tiled=True)  172 us
    reduce_sum x1, other arithmetic, shards(): jnp.sum(jnp.where(query_ids[:, :, None] == columns[None, None, :], weight...  17.3 us
    all_to_all x1, starting transfers between devices, shards(): lax.all_to_all(jnp.stack([patches] * lax.axis_size('term')), 'term', 0, 0)  15.5 us
  transfers between devices with their start and end apart: 3, of which 1 were waited for; matrix products, arithmetic and copies ran while one was open for 4% of the time, Pallas kernels for 0%

profile of v1, /device:TPU:24, one launch (start us, length us, event | category | flops | bytes accessed | tf_op | source)
XLA Modules:
  0.0 482.9 jit_solution(4892524763893936108)
XLA Ops:
  6.5 2.4 stack.2
  8.9 0.0 copy-start.2
  8.9 0.0 copy-start
  8.9 0.0 copy-start.1
  8.9 15.5 %all-to-all-start = ((bf16[32,4,8,1024]{3,2,1,0:T(8,128)(2,1)}), bf16[32,4,8,1024]{3,2,1,0:T(8,128)(2,1)S(1)}, u32[]{:S(2)}, u32[]{:S(2)}) async-start(bf16[32,4,8,1024]{3,2,1,0:T(8,128)(2,1)} %stack.2), calls=%async_computation | async-start | bytes 4194304 | tf_op jit(solution)/shard_map/all_to_all | solution.py:12
  24.5 0.0 copy-start.4
  24.5 0.0 all-gather.3.cloned.1.call-start
  24.5 0.7 all-gather.3.cloned.1.call-update
  25.2 0.0 reduce-scatter.2.cloned.1.call-start
  25.3 0.0 copy-done.2
  25.3 171.7 %all-gather = bf16[32,8,4]{1,2,0:T(4,128)(2,1)S(1)} all-gather(bf16[1,8,4]{1,2,0:T(4,128)(2,1)S(1)} %convert_bitcast_fusion), channel_id=1, replica_groups=mesh['img'=16,'term'=32] {'term'}, dimensions={0}, use_global_device_ids=true | all-gather | bytes 2112 | tf_op jit(solution)/shard_map/all_gather | solution.py:14
  197.0 0.1 copy.26
  197.1 0.1 copy.27
  197.2 0.1 reshape.22
  197.3 0.0 copy-done
  197.3 0.0 copy-done.1
  197.4 17.3 %fusion = bf16[1024,960]{0,1:T(8,128)(2,1)} fusion(s32[1024,32]{0,1:T(8,128)S(1)} %copy-done, s32[960]{0:T(1024)S(1)} %iota_add_fusion, bf16[1024,32]{0,1:T(8,128)(2,1)S(1)} %compare_select_fusion.1), kind=kLoop, calls=%fused_computation.1 | loop fusion | flops 93388800 | bytes 2166528 | tf_op jit(solution)/shard_map/reduce_sum | solution.py:27
  214.7 0.0 all-gather.3.cloned.1.call-done
  214.7 0.0 all-to-all-done
  214.7 0.0 copy-done.4
  214.7 0.0 copy-start.3
  214.7 5.5 %select_reduce_fusion = bf16[4,960]{1,0:T(4,128)(2,1)S(1)} fusion(f32[960]{0:T(1024)S(1)} %copy-done.4, pred[4,256]{1,0:T(4,128)(4,1)S(1)} %bitcast.20, bf16[1024,960]{1,0:T(8,128)(2,1)} %all-gather.3.cloned.1.call-done, bf16[32,4,8,1024]{3,2,1,0:T(8,128)(2,1)S(1)} %all-to-all-done), kind=kOutput, calls=%fused_computation.2 | convolution fusion | flops 2017194240 | bytes 4075776 | tf_op jit(solution)/shard_map/npd,dv->npv/dot_general | solution.py:16
  220.2 0.2 copy.29
  220.4 0.0 copy-done.3
  220.4 4.2 fusion.9
  224.7 0.0 reduce-scatter.2.cloned.1.call-update
  224.7 251.4 %reduce-scatter.2.cloned.1.call-done = f32[32,512]{1,0:T(8,128)} async-done(((f32[1024,512]{1,0:T(8,128)}), f32[32,512]{1,0:T(8,128)}) %reduce-scatter.2.cloned.1.call-update) | async-done | bytes 65552 | tf_op jit(solution)/shard_map/reduce_scatter | solution.py:31
  (5 shorter events, 0.0 us)
Async XLA Ops:
  8.9 16.3 %copy-start.2 = (s32[4,8]{1,0:T(4,128)S(1)}, s32[4,8]{1,0:T(4,128)}, u32[]{:S(2)}) copy-start(s32[4,8]{1,0:T(4,128)} %param.8) | copy-start | bytes 388
  8.9 188.4 %copy-start = (s32[1024,32]{0,1:T(8,128)S(1)}, s32[1024,32]{0,1:T(8,128)}, u32[]{:S(2)}) copy-start(s32[1024,32]{0,1:T(8,128)} %param.12) | copy-start | bytes 393220
  8.9 188.4 %copy-start.1 = (bf16[1024,32]{0,1:T(8,128)(2,1)S(1)}, bf16[1024,32]{0,1:T(8,128)(2,1)}, u32[]{:S(2)}) copy-start(bf16[1024,32]{0,1:T(8,128)(2,1)} %param.13) | copy-start | bytes 196612
  8.9 205.7 %all-to-all-start = ((bf16[32,4,8,1024]{3,2,1,0:T(8,128)(2,1)}), bf16[32,4,8,1024]{3,2,1,0:T(8,128)(2,1)S(1)}, u32[]{:S(2)}, u32[]{:S(2)}) async-start(bf16[32,4,8,1024]{3,2,1,0:T(8,128)(2,1)} %stack.2), calls=%async_computation | async-start | bytes 4194304 | tf_op jit(solution)/shard_map/all_to_all | solution.py:12
  24.5 190.2 %copy-start.4 = (f32[960]{0:T(1024)S(1)}, f32[960]{0:T(1024)}, u32[]{:S(2)}) copy-start(f32[960]{0:T(1024)} %param.10) | copy-start | bytes 11524
  24.5 190.2 %all-gather.3.cloned.1.call-start = ((), (), s32[]{:S(2)}) async-start(), calls=%async_computation.2 | async-start | bytes 2228224 | tf_op jit(solution)/shard_map/all_gather | solution.py:8
  25.2 450.9 %reduce-scatter.2.cloned.1.call-start = ((), (), s32[]{:S(2)}) async-start(), calls=%async_computation.3 | async-start | bytes 2162688 | tf_op jit(solution)/shard_map/reduce_scatter | solution.py:31
  214.7 5.7 %copy-start.3 = (bf16[508,960]{0,1:T(8,128)(2,1)S(1)}, bf16[508,960]{0,1:T(8,128)(2,1)}, u32[]{:S(2)}) copy-start(bf16[508,960]{0,1:T(8,128)(2,1)} %param.11) | copy-start | bytes 2926084
Sparse Core Ops, SparseCore 0:
  28.6 98.7 all-gather.2
  224.8 251.2 reduce-scatter.1
